TPU v7x, 512 devices: a whole 4x4x16 slice. The times are simulated.
512 devices in a mesh: rows: 128 (over x, z, core), rep: 4 (over y).
Axes of the slice: x: 4, y: 4, z: 16, core: 2. Of those that a mesh axis runs over, the one named last changes fastest.
Arguments:
- feats: bfloat16 [4, 32768, 512], P('rep', 'rows'), may hold values from -24 to 24
- grad_out: bfloat16 [4, 32768, 512], P('rep', 'rows'), may hold values from -6 to 6
- qkv_weight: bfloat16 [512, 1536], P('rows'), may hold values from -0.25 to 0.25
- proj_weight: bfloat16 [512, 512], P('rows'), may hold values from -0.25 to 0.25
- to_hilbert: int32 [4, 16384], P('rep', 'rows'), may hold values from 0 to 16383, as said below
- to_zorder: int32 [4, 16384], P('rep', 'rows'), may hold values from 0 to 16383, as said below
Outputs:
- grad_feats: bfloat16 [4, 32768, 512], P('rep', 'rows')
- qkv_grad: float32 [512, 1536], P('rows')
- proj_grad: float32 [512, 512], P('rows')
Inputs may be any that keep to these rules, and one draw needn't show every extreme that they name: to_hilbert[s] is a permutation of the blocks of scene s and to_zorder[s] its inverse; of the 128 Z-order blocks of one device, at most 2 have Hilbert positions on any one device, and exactly 2 for some pair of devices in every scene. `to_zorder`: the inverse of to_hilbert in every scene.
All inputs are finite; a program needn't handle non-finite values.
Results may differ from a plain program's by a relative error of at most 0.015.
The roundings to bfloat16 on the way count: a program that leaves them out, or rounds other values in their place, can miss the bound.
Values may be sent and summed in bfloat16 or wider, within the bound.
No kernel may reach another device: no remote copies, remote signals or barrier semaphores. Data moves between devices by JAX's collectives and lax.ppermute only.
A program may use at most 64 MiB of HBM per device.

v0:
```python
import jax
import jax.numpy as jnp
from jax import lax
from jax.sharding import PartitionSpec as P

HEADS = 8
CAP = 2


def from_partner(block, axis, apart):
    count = lax.axis_size(axis)
    route = []
    for low in range(count):
        high = low | 1 << apart
        if high != low and high < count:
            route += [(low, high), (high, low)]
    return lax.ppermute(block, axis, route)


def move_blocks(outgoing):
    return lax.all_to_all(outgoing, "rows", split_axis=0, concat_axis=0, tiled=True)


def rank_within(order_keys, owners):
    same_owner = owners[None, :] == owners[:, None]
    earlier = order_keys[None, :] < order_keys[:, None]
    return jnp.sum(jnp.logical_and(same_owner, earlier).astype(jnp.int32), axis=1)


def contract_rows(left, right):
    return lax.dot_general(
        left, right, (((0,), (0,)), ((), ())), preferred_element_type=jnp.float32
    )


def contract_cols(left, right):
    return lax.dot_general(
        left, right, (((1,), (1,)), ((), ())), preferred_element_type=jnp.float32
    )


def per_device(feats, grad_out, qkv_weight, proj_weight, to_hilbert, to_zorder):
    peer_count = lax.axis_size("rows")
    feature = feats[0]
    rows_dev, channels = feature.shape
    head_size = channels // HEADS
    scale = head_size ** (-0.5)
    blocks_dev = to_hilbert.shape[1]
    slot_count = peer_count * CAP
    w_qkv, w_proj = (
        lax.all_gather(qkv_weight, "rows", axis=0, tiled=True),
        lax.all_gather(proj_weight, "rows", axis=0, tiled=True),
    )
    forward_list = to_hilbert[0]
    inverse_list = to_zorder[0]
    local_ids = jnp.arange(blocks_dev, dtype=jnp.int32)
    slot_ids = jnp.arange(slot_count, dtype=jnp.int32)
    target_dev = forward_list // blocks_dev
    send_slot = target_dev * CAP + rank_within(local_ids, target_dev)
    send_table = (send_slot[None, :] == slot_ids[:, None]).astype(jnp.bfloat16)
    source_dev = inverse_list // blocks_dev
    recv_slot = source_dev * CAP + rank_within(inverse_list, source_dev)
    recv_table = (recv_slot[:, None] == slot_ids[None, :]).astype(jnp.bfloat16)
    zblocks = grad_out[0].reshape(blocks_dev, -1)
    outgoing = jnp.dot(send_table, zblocks, preferred_element_type=jnp.float32).astype(jnp.bfloat16)
    arrived = move_blocks(outgoing.reshape(peer_count, CAP, -1)).reshape(slot_count, -1)
    grad_hil = jnp.dot(recv_table, arrived, preferred_element_type=jnp.float32).astype(jnp.bfloat16)
    grad_hil = grad_hil.reshape(rows_dev, channels)
    qkv = jnp.dot(feature, w_qkv, preferred_element_type=jnp.float32).astype(jnp.bfloat16)
    query = qkv[:, :channels]
    keyval = qkv[:, channels:]
    grad_attn = contract_cols(grad_hil, w_proj).astype(jnp.bfloat16)
    other_kv = from_partner(keyval, "rows", 0)
    keys_all = jnp.concatenate([keyval[:, :channels], other_kv[:, :channels]], axis=0)
    values_all = jnp.concatenate([keyval[:, channels:], other_kv[:, channels:]], axis=0)
    attn_parts, dq_parts, dk_parts, dv_parts = ([], [], [], [])
    for head_index in range(HEADS):
        lo_col = head_index * head_size
        q_head = query[:, lo_col : lo_col + head_size]
        k_head = keys_all[:, lo_col : lo_col + head_size]
        v_head = values_all[:, lo_col : lo_col + head_size]
        g_head = grad_attn[:, lo_col : lo_col + head_size]
        score = contract_cols(q_head, k_head) * scale
        row_max = jnp.max(score, axis=1, keepdims=True)
        raised = jnp.exp(score - row_max)
        row_sum = jnp.sum(raised, axis=1, keepdims=True)
        probs = raised / row_sum
        probs_b = probs.astype(jnp.bfloat16)
        attn_parts.append(
            jnp.dot(probs_b, v_head, preferred_element_type=jnp.float32).astype(jnp.bfloat16)
        )
        dprob = contract_cols(g_head, v_head)
        delta = jnp.sum(probs * dprob, axis=1, keepdims=True)
        dscore = (probs * (dprob - delta) * scale).astype(jnp.bfloat16)
        dq_parts.append(jnp.dot(dscore, k_head, preferred_element_type=jnp.float32))
        dk_parts.append(contract_rows(dscore, q_head))
        dv_parts.append(contract_rows(probs_b, g_head))
    grad_q = jnp.concatenate(dq_parts, axis=1)
    grad_k = jnp.concatenate(dk_parts, axis=1)
    grad_v = jnp.concatenate(dv_parts, axis=1)
    other_k, other_v = (
        from_partner(grad_k[rows_dev:].astype(jnp.bfloat16), "rows", 0).astype(jnp.float32),
        from_partner(grad_v[rows_dev:].astype(jnp.bfloat16), "rows", 0).astype(jnp.float32),
    )
    grad_k = grad_k[:rows_dev] + other_k
    grad_v = grad_v[:rows_dev] + other_v
    grad_qkv = jnp.concatenate([grad_q, grad_k, grad_v], axis=1).astype(jnp.bfloat16)
    attn = jnp.concatenate(attn_parts, axis=1)
    grad_hfeat = contract_cols(grad_qkv, w_qkv).astype(jnp.bfloat16)
    hblocks = grad_hfeat.reshape(blocks_dev, -1)
    going_back = contract_rows(recv_table, hblocks).astype(jnp.bfloat16)
    returned = move_blocks(going_back.reshape(peer_count, CAP, -1)).reshape(slot_count, -1)
    grad_z = contract_rows(send_table, returned).astype(jnp.bfloat16).reshape(rows_dev, channels)
    share = channels // peer_count
    term = jnp.concatenate(
        [contract_rows(feature, grad_qkv), contract_rows(attn, grad_hil)], axis=1
    )
    total = lax.psum(term, ("rows", "rep"))
    owned = lax.dynamic_slice_in_dim(total, lax.axis_index("rows") * share, share, 0)
    return (grad_z[None], owned[:, : 3 * channels], owned[:, 3 * channels :])


def solution(mesh):
    placed = (
        P("rep", "rows", None),
        P("rep", "rows", None),
        P("rows", None),
        P("rows", None),
        P("rep", "rows"),
        P("rep", "rows"),
    )
    return jax.shard_map(
        per_device,
        mesh=mesh,
        in_specs=placed,
        out_specs=(P("rep", "rows", None), P("rows", None), P("rows", None)),
        check_vma=False,
    )
```

profile of v0, /device:TPU:2, one launch (start us, length us, event | category | flops | bytes accessed | tf_op | source)
XLA Modules:
  0.0 721.0 jit_solution(14029525855574183305)
XLA Ops:
  7.9 1.0 reshape_squeeze.3
  11.5 1.0 reshape.119
  12.5 19.5 %all-to-all-start = ((bf16[128,2,1024]{2,1,0:T(2,128)(2,1)}), bf16[128,2,1024]{2,1,0:T(2,128)(2,1)S(1)}, u32[]{:S(2)}, u32[]{:S(2)}) async-start(bf16[128,2,1024]{2,1,0:T(2,128)(2,1)} %reshape.119), calls=%async_computation | async-start | bytes 1048576 | tf_op jit(solution)/shard_map/all_to_all | solution.py:21
  32.0 100.5 %all-gather.1 = bf16[128,4,512]{2,1,0:T(4,128)(2,1)S(1)} all-gather(bf16[1,4,512]{2,1,0:T(4,128)(2,1)S(1)} %bitcast.64), channel_id=1, replica_groups=mesh['rows'=128,'rep'=4] {'rows'}, dimensions={0}, use_global_device_ids=true | all-gather | bytes 528384 | tf_op jit(solution)/shard_map/all_gather | solution.py:52
  132.9 1.0 reshape.120
  133.9 22.9 %all-gather.4.cloned.1.call-done = bf16[128,4,1536]{2,1,0:T(4,128)(2,1)} async-done(((bf16[1,4,1536]{2,1,0:T(4,128)(2,1)}), bf16[128,4,1536]{2,1,0:T(4,128)(2,1)}) %all-gather.4.cloned.1.call-update) | async-done | bytes 1572880 | tf_op jit(solution)/shard_map/all_gather | solution.py:51
  156.9 2.7 reshape.126
  161.0 2.3 collective-permute-start
  164.4 1.0 reshape.121
  165.8 1.1 fusion.160
  180.5 2.1 collective-permute-start.2
  182.6 1.3 fusion.169
  188.6 2.4 collective-permute-start.1
  192.2 1.3 convolution_convert_fusion.4
  194.1 1.7 reshape.122
  195.8 2.2 convolution_convert_fusion.1
  198.0 2.1 reshape.123
  200.1 12.8 %all-to-all-start.1 = ((bf16[128,2,1024]{2,1,0:T(2,128)(2,1)}), bf16[128,2,1024]{2,1,0:T(2,128)(2,1)}, u32[]{:S(2)}, u32[]{:S(2)}) async-start(bf16[128,2,1024]{2,1,0:T(2,128)(2,1)} %reshape.123), calls=%async_computation.1 | async-start | bytes 1048576 | tf_op jit(solution)/shard_map/all_to_all | solution.py:21
  212.9 3.6 pad_maximum_fusion
  216.5 29.6 %all-to-all-done.1 = bf16[128,2,1024]{2,1,0:T(2,128)(2,1)} async-done(((bf16[128,2,1024]{2,1,0:T(2,128)(2,1)}), bf16[128,2,1024]{2,1,0:T(2,128)(2,1)}, u32[]{:S(2)}, u32[]{:S(2)}) %all-to-all-start.1) | async-done | bytes 524320 | tf_op jit(solution)/shard_map/all_to_all | solution.py:21
  246.2 1.2 reshape.124
  248.5 461.6 %all-reduce.2.cloned.1.call-done = f32[512,2048]{0,1:T(8,128)} async-done(((f32[512,2048]{0,1:T(8,128)}), f32[512,2048]{0,1:T(8,128)}) %all-reduce.2.cloned.1.call-update) | async-done | bytes 4194320 | tf_op jit(solution)/shard_map/psum | solution.py:118
  710.0 1.4 constant_dynamic-slice_fusion
  712.3 1.1 dynamic-slice.1
  (106 shorter events, 28.9 us)
Async XLA Ops:
  7.2 152.4 %copy-start = (bf16[1,256,512]{2,1,0:T(8,128)(2,1)S(1)}, bf16[1,256,512]{2,1,0:T(8,128)(2,1)}, u32[]{:S(2)}) copy-start(bf16[1,256,512]{2,1,0:T(8,128)(2,1)} %param.6) | copy-start | bytes 786436
  7.2 24.8 %copy-start.2 = (bf16[4,512]{1,0:T(4,128)(2,1)S(1)}, bf16[4,512]{1,0:T(4,128)(2,1)}, u32[]{:S(2)}) copy-start(bf16[4,512]{1,0:T(4,128)(2,1)} %param.9) | copy-start | bytes 12292
  7.2 125.5 %copy-start.3 = (s32[1,128]{1,0:T(1,128)S(1)}, s32[1,128]{1,0:T(1,128)}, u32[]{:S(2)}) copy-start(s32[1,128]{1,0:T(1,128)} %param.11) | copy-start | bytes 1540
  7.2 149.7 %all-gather.4.cloned.1.call-start = ((), (), s32[]{:S(2)}) async-start(), calls=%async_computation.3 | async-start | bytes 1585152 | tf_op jit(solution)/shard_map/all_gather | solution.py:51
  12.5 120.5 %all-to-all-start = ((bf16[128,2,1024]{2,1,0:T(2,128)(2,1)}), bf16[128,2,1024]{2,1,0:T(2,128)(2,1)S(1)}, u32[]{:S(2)}, u32[]{:S(2)}) async-start(bf16[128,2,1024]{2,1,0:T(2,128)(2,1)} %reshape.119), calls=%async_computation | async-start | bytes 1048576 | tf_op jit(solution)/shard_map/all_to_all | solution.py:21
  159.6 3.8 copy-start.1
  161.0 4.8 collective-permute-start
  180.5 11.7 %collective-permute-start.2 = (bf16[256,512]{0,1:T(8,128)(2,1)S(1)}, bf16[256,512]{0,1:T(8,128)(2,1)S(1)}, u32[]{:S(2)}, u32[]{:S(2)}) collective-permute-start(bf16[256,512]{0,1:T(8,128)(2,1)S(1)} %slice.454), channel_id=1, source_target_pairs={{0,4},{4,0},{8,12},{12,8},{16,20},{20,16},{24,28},{28,24},{32,36},... | collective-permute-start | bytes 786440 | tf_op jit(solution)/shard_map/ppermute | solution.py:17
  188.6 3.4 collective-permute-start.1
  200.1 46.1 %all-to-all-start.1 = ((bf16[128,2,1024]{2,1,0:T(2,128)(2,1)}), bf16[128,2,1024]{2,1,0:T(2,128)(2,1)}, u32[]{:S(2)}, u32[]{:S(2)}) async-start(bf16[128,2,1024]{2,1,0:T(2,128)(2,1)} %reshape.123), calls=%async_computation.1 | async-start | bytes 1048576 | tf_op jit(solution)/shard_map/all_to_all | solution.py:21
  212.9 497.2 %all-reduce.2.cloned.1.call-start = ((), (), s32[]{:S(2)}) async-start(), calls=%async_computation.2 | async-start | bytes 8388608 | tf_op jit(solution)/shard_map/psum | solution.py:118
Sparse Core Ops, SparseCore 0:
  11.1 145.7 all-gather.3
  219.2 490.8 all-reduce.1
where the time goes:
time: 722 us; the launch traced here: 721 us
  waiting for transfers between devices  515 us (71%)
  blocking collectives  101 us (14%)
  starting transfers between devices  39.3 us (5%)
  matrix products  22.5 us (3%)
  local copies, waits for them, and re-layouts  18.9 us (3%)
  between operations  14.4 us (2%)
  other arithmetic  9.94 us (1%)
    psum x1, waiting for transfers between devices, per_device(): total = lax.psum(term, ('rows', 'rep'))  462 us
    all_gather x1, blocking collectives, per_device(): lax.all_gather(proj_weight, 'rows', axis=0, tiled=True)  101 us
    all_to_all x2, starting transfers between devices, move_blocks(): lax.all_to_all(outgoing, 'rows', split_axis=0, concat_axis=0, tiled=True)  32.3 us
    all_to_all x2, waiting for transfers between devices, move_blocks(): lax.all_to_all(outgoing, 'rows', split_axis=0, concat_axis=0, tiled=True)  29.6 us
    all_gather x1, waiting for transfers between devices, per_device(): lax.all_gather(qkv_weight, 'rows', axis=0, tiled=True)  22.9 us
  transfers between devices with their start and end apart: 7, of which 4 were waited for; matrix products, arithmetic and copies ran while one was open for 3% of the time, Pallas kernels for 0%

commit v1 on v0

--- a/solution.py
+++ b/solution.py
@@ -115,7 +115,7 @@
     term = jnp.concatenate(
         [contract_rows(feature, grad_qkv), contract_rows(attn, grad_hil)], axis=1
     )
-    total = lax.psum(term, ("rows", "rep"))
+    total = lax.psum(lax.psum(term, "rep"), "rows")
     owned = lax.dynamic_slice_in_dim(total, lax.axis_index("rows") * share, share, 0)
     return (grad_z[None], owned[:, : 3 * channels], owned[:, 3 * channels :])
 

time: 722 us -> 674 us (0.934)
  the two profiles are of different devices: /device:TPU:2 before, /device:TPU:8 now
where the time goes in v1:
time: 674 us
  waiting for transfers between devices  476 us (71%)
  blocking collectives  100 us (15%)
  starting transfers between devices  38.4 us (6%)
  matrix products  19 us (3%)
  local copies, waits for them, and re-layouts  17.2 us (3%)
  between operations  14.2 us (2%)
  other arithmetic  8.77 us (1%)
    psum x2, waiting for transfers between devices, per_device(): total = lax.psum(lax.psum(term, 'rep'), 'rows')  451 us
    all_gather x1, blocking collectives, per_device(): lax.all_gather(proj_weight, 'rows', axis=0, tiled=True)  100 us
    all_to_all x2, starting transfers between devices, move_blocks(): lax.all_to_all(outgoing, 'rows', split_axis=0, concat_axis=0, tiled=True)  31.4 us
    all_gather x1, waiting for transfers between devices, per_device(): lax.all_gather(qkv_weight, 'rows', axis=0, tiled=True)  23.7 us
  transfers between devices with their start and end apart: 8, of which 4 were waited for; matrix products, arithmetic and copies ran while one was open for 3% of the time, Pallas kernels for 0%

profile of v1, /device:TPU:8, one launch (start us, length us, event | category | flops | bytes accessed | tf_op | source)
XLA Modules:
  0.0 673.5 jit_solution(1191052155098083015)
XLA Ops:
  7.9 1.0 reshape_squeeze.3
  11.5 1.0 reshape.119
  12.5 19.8 %all-to-all-start = ((bf16[128,2,1024]{2,1,0:T(2,128)(2,1)}), bf16[128,2,1024]{2,1,0:T(2,128)(2,1)S(1)}, u32[]{:S(2)}, u32[]{:S(2)}) async-start(bf16[128,2,1024]{2,1,0:T(2,128)(2,1)} %reshape.119), calls=%async_computation | async-start | bytes 1048576 | tf_op jit(solution)/shard_map/all_to_all | solution.py:21
  32.3 100.3 %all-gather.1 = bf16[128,4,512]{2,1,0:T(4,128)(2,1)S(1)} all-gather(bf16[1,4,512]{2,1,0:T(4,128)(2,1)S(1)} %bitcast.64), channel_id=1, replica_groups=mesh['rows'=128,'rep'=4] {'rows'}, dimensions={0}, use_global_device_ids=true | all-gather | bytes 528384 | tf_op jit(solution)/shard_map/all_gather | solution.py:52
  133.0 1.0 reshape.120
  134.0 23.7 %all-gather.4.cloned.1.call-done = bf16[128,4,1536]{2,1,0:T(4,128)(2,1)} async-done(((bf16[1,4,1536]{2,1,0:T(4,128)(2,1)}), bf16[128,4,1536]{2,1,0:T(4,128)(2,1)}) %all-gather.4.cloned.1.call-update) | async-done | bytes 1572880 | tf_op jit(solution)/shard_map/all_gather | solution.py:51
  157.7 2.7 reshape.126
  161.0 0.9 slice.187
  161.9 2.3 collective-permute-start
  164.3 1.0 convolution_convert_fusion.6
  165.2 1.0 reshape.121
  166.7 1.1 fusion.160
  181.3 2.1 collective-permute-start.2
  188.5 2.4 collective-permute-start.1
  192.1 0.9 copy-done.2
  193.6 2.4 pad_maximum_fusion
  196.1 1.1 copy-done.3
  198.3 1.0 reshape.123
  199.3 11.7 %all-to-all-start.1 = ((bf16[128,2,1024]{2,1,0:T(2,128)(2,1)}), bf16[128,2,1024]{2,1,0:T(2,128)(2,1)S(1)}, u32[]{:S(2)}, u32[]{:S(2)}) async-start(bf16[128,2,1024]{2,1,0:T(2,128)(2,1)} %reshape.123), calls=%async_computation.1 | async-start | bytes 1048576 | tf_op jit(solution)/shard_map/all_to_all | solution.py:21
  211.1 88.4 %all-reduce.3.cloned.1.call-done = f32[512,2048]{0,1:T(8,128)} async-done(((f32[512,2048]{0,1:T(8,128)}), f32[512,2048]{0,1:T(8,128)}) %all-reduce.3.cloned.1.call-update) | async-done | bytes 4194320 | tf_op jit(solution)/shard_map/psum | solution.py:118
  300.8 362.2 %all-reduce.5.cloned.1.call-done = f32[512,2048]{0,1:T(8,128)} async-done(((f32[512,2048]{0,1:T(8,128)}), f32[512,2048]{0,1:T(8,128)}) %all-reduce.5.cloned.1.call-update) | async-done | bytes 4194320 | tf_op jit(solution)/shard_map/psum | solution.py:118
  662.9 1.4 constant_dynamic-slice_fusion
  664.3 0.9 copy.13
  665.2 1.1 dynamic-slice.1
  (113 shorter events, 27.9 us)
Async XLA Ops:
  7.2 153.3 %copy-start = (bf16[1,256,512]{2,1,0:T(8,128)(2,1)S(1)}, bf16[1,256,512]{2,1,0:T(8,128)(2,1)}, u32[]{:S(2)}) copy-start(bf16[1,256,512]{2,1,0:T(8,128)(2,1)} %param.6) | copy-start | bytes 786436
  7.2 25.1 %copy-start.4 = (bf16[4,512]{1,0:T(4,128)(2,1)S(1)}, bf16[4,512]{1,0:T(4,128)(2,1)}, u32[]{:S(2)}) copy-start(bf16[4,512]{1,0:T(4,128)(2,1)} %param.9) | copy-start | bytes 12292
  7.2 125.6 %copy-start.5 = (s32[1,128]{1,0:T(1,128)S(1)}, s32[1,128]{1,0:T(1,128)}, u32[]{:S(2)}) copy-start(s32[1,128]{1,0:T(1,128)} %param.11) | copy-start | bytes 1540
  7.2 150.5 %all-gather.4.cloned.1.call-start = ((), (), s32[]{:S(2)}) async-start(), calls=%async_computation.4 | async-start | bytes 1585152 | tf_op jit(solution)/shard_map/all_gather | solution.py:51
  12.5 120.6 %all-to-all-start = ((bf16[128,2,1024]{2,1,0:T(2,128)(2,1)}), bf16[128,2,1024]{2,1,0:T(2,128)(2,1)S(1)}, u32[]{:S(2)}, u32[]{:S(2)}) async-start(bf16[128,2,1024]{2,1,0:T(2,128)(2,1)} %reshape.119), calls=%async_computation | async-start | bytes 1048576 | tf_op jit(solution)/shard_map/all_to_all | solution.py:21
  32.3 267.2 %all-reduce.3.cloned.1.call-start = ((), (), s32[]{:S(2)}) async-start(), calls=%async_computation.2 | async-start | bytes 8388608 | tf_op jit(solution)/shard_map/psum | solution.py:118
  160.5 3.8 copy-start.1
  161.9 4.8 collective-permute-start
  181.3 10.7 %collective-permute-start.2 = (bf16[256,512]{0,1:T(8,128)(2,1)S(1)}, bf16[256,512]{0,1:T(8,128)(2,1)S(1)}, u32[]{:S(2)}, u32[]{:S(2)}) collective-permute-start(bf16[256,512]{0,1:T(8,128)(2,1)S(1)} %slice.454), channel_id=1, source_target_pairs={{0,4},{4,0},{8,12},{12,8},{16,20},{20,16},{24,28},{28,24},{32,36},... | collective-permute-start | bytes 786440 | tf_op jit(solution)/shard_map/ppermute | solution.py:17
  188.5 3.4 collective-permute-start.1
  192.1 0.9 copy-start.2
  196.0 1.1 copy-start.3
  199.3 100.2 %all-to-all-start.1 = ((bf16[128,2,1024]{2,1,0:T(2,128)(2,1)}), bf16[128,2,1024]{2,1,0:T(2,128)(2,1)S(1)}, u32[]{:S(2)}, u32[]{:S(2)}) async-start(bf16[128,2,1024]{2,1,0:T(2,128)(2,1)} %reshape.123), calls=%async_computation.1 | async-start | bytes 1048576 | tf_op jit(solution)/shard_map/all_to_all | solution.py:21
  211.0 451.9 %all-reduce.5.cloned.1.call-start = ((), (), s32[]{:S(2)}) async-start(), calls=%async_computation.3 | async-start | bytes 8388608 | tf_op jit(solution)/shard_map/psum | solution.py:118
Sparse Core Ops, SparseCore 0:
  11.1 146.5 all-gather.3
  196.2 103.2 all-reduce.2
  303.3 359.5 all-reduce.4
